TPU v7x, 32 devices: a whole 2x2x4 slice. The times are simulated.
32 devices in a mesh: scene: 4 (over y, core), frame: 8 (over z, x).
Axes of the slice: x: 2, y: 2, z: 4, core: 2. Of those that a mesh axis runs over, the one named last changes fastest.
Arguments:
- occupancy: bfloat16 [4, 32, 64, 2048], P('scene', 'frame'), may hold values from -6 to 6
- scene_lengths: int32 [4], P('scene'), may hold values from 8 to 32, as said below
- conv1_weight: bfloat16 [128, 1728], replicated, may hold values from -0.15625 to 0.15625
- conv2_weight: bfloat16 [256, 3456], replicated, may hold values from -0.109375 to 0.109375
- temporal_weight: bfloat16 [3, 256, 256], replicated, may hold values from -0.21875 to 0.21875
- query_weight: bfloat16 [256, 256], replicated
- key_weight: bfloat16 [256, 256], replicated
- value_weight: bfloat16 [256, 256], replicated, may hold values from -0.375 to 0.375
- out_weight: bfloat16 [256, 256], replicated, may hold values from -0.375 to 0.375
Outputs:
- encoded: bfloat16 [4, 32, 256, 512], P('scene', 'frame')
- kl_loss: float32 [], replicated
Inputs may be any that keep to these rules, and one draw needn't show every extreme that they name: `scene_lengths`: non-decreasing along the scenes; the first scene has exactly 8 frames with data and the last exactly 32.
All inputs are finite; a program needn't handle non-finite values.
Results may differ from a plain program's by a relative error of at most 0.011.
Values may be sent and summed in bfloat16 or wider, within the bound.
No kernel may reach another device: no remote copies, remote signals or barrier semaphores. Data moves between devices by JAX's collectives and lax.ppermute only.
A program may use at most 192 MiB of HBM per device.

v0:
```python
import jax
import jax.numpy as jnp
from jax import lax
from jax.sharding import PartitionSpec as P

CIN = 64
C1 = 128
C2 = 256
HEADS = 4
HD = 64
HI = 16
ZD = 8
CELLS = 512
NORM_EPS = 1e-06


def spatial_conv(voxels, weight, channels_in, stride):
    channels_out = weight.shape[0]
    kernel = weight.reshape(channels_out, channels_in, 3, 3, 3)
    return lax.conv_general_dilated(
        voxels,
        kernel,
        (stride, stride, 1),
        ((1, 1), (1, 1), (1, 1)),
        dimension_numbers=("NCDHW", "OIDHW", "NCDHW"),
        preferred_element_type=jnp.float32,
    )


def mix_channels(weight, maps):
    return jnp.einsum("oc,fcn->fon", weight, maps, preferred_element_type=jnp.float32)


def temporal_block(padded, second_maps, temporal_weight):
    count_frames = second_maps.shape[0]
    temporal_sum = mix_channels(temporal_weight[0], padded[0:count_frames])
    for tap in range(1, 3):
        temporal_sum = temporal_sum + mix_channels(
            temporal_weight[tap], padded[tap : tap + count_frames]
        )
    residual_maps = (second_maps.astype(jnp.float32) + jax.nn.silu(temporal_sum)).astype(
        jnp.bfloat16
    )
    return residual_maps.astype(jnp.float32)


def project_rows(residual_f, query_weight, key_weight, value_weight):
    count_frames = residual_f.shape[0]
    count_cells = residual_f.shape[2]
    normed = (
        residual_f * lax.rsqrt(jnp.mean(residual_f * residual_f, axis=1, keepdims=True) + NORM_EPS)
    ).astype(jnp.bfloat16)
    queries = (
        mix_channels(query_weight, normed)
        .astype(jnp.bfloat16)
        .reshape(count_frames, HEADS, HD, count_cells)
    )
    key_rows = (
        mix_channels(key_weight, normed)
        .astype(jnp.bfloat16)
        .reshape(count_frames, HEADS, HD, count_cells)
    )
    value_rows = (
        mix_channels(value_weight, normed)
        .astype(jnp.bfloat16)
        .reshape(count_frames, HEADS, HD, count_cells)
    )
    return (queries, key_rows, value_rows)


def finish_rows(residual_f, attended, out_weight, valid_rows):
    count_frames = residual_f.shape[0]
    count_cells = residual_f.shape[2]
    out_full = residual_f + mix_channels(
        out_weight, attended.reshape(count_frames, C2, count_cells)
    )
    return (out_full * valid_rows[:, None, None]).astype(jnp.bfloat16)


def attend_whole(queries, key_rows, value_rows, length):
    scores = jnp.einsum(
        "qhdc,khdc->qkhc", queries, key_rows, preferred_element_type=jnp.float32
    ) * HD ** (-0.5)
    key_mask = (jnp.arange(key_rows.shape[0]) < length)[None, :, None, None]
    scores = jnp.where(key_mask, scores, -1e30)
    row_max = jnp.max(scores, axis=1, keepdims=True)
    raw_weights = jnp.where(key_mask, jnp.exp(scores - row_max), 0.0)
    row_total = jnp.sum(raw_weights, axis=1)
    weighted = jnp.einsum(
        "qkhc,khdc->qhdc",
        raw_weights.astype(jnp.bfloat16),
        value_rows,
        preferred_element_type=jnp.float32,
    )
    return (weighted / row_total[:, :, None, :]).astype(jnp.bfloat16)


def shards(
    occupancy,
    scene_lengths,
    conv1_weight,
    conv2_weight,
    temporal_weight,
    query_weight,
    key_weight,
    value_weight,
    out_weight,
):
    f_dev = occupancy.shape[1]
    length = scene_lengths[0]
    first_frame = lax.axis_index("frame") * f_dev
    frame_ids = first_frame + jnp.arange(f_dev, dtype=jnp.int32)
    valid_rows = (frame_ids < length).astype(jnp.float32)
    voxels = occupancy[0].reshape(f_dev, CIN, HI, HI, ZD)
    first_maps = jax.nn.silu(spatial_conv(voxels, conv1_weight, CIN, 2)).astype(jnp.bfloat16)
    second_full = jax.nn.silu(spatial_conv(first_maps, conv2_weight, C1, 1))
    second_maps = (second_full.reshape(f_dev, C2, CELLS) * valid_rows[:, None, None]).astype(
        jnp.bfloat16
    )
    cell_maps = lax.all_to_all(second_maps, "frame", split_axis=2, concat_axis=0, tiled=True)
    frames_all = cell_maps.shape[0]
    padded_all = jnp.pad(cell_maps, ((1, 1), (0, 0), (0, 0)))
    residual_cols = temporal_block(padded_all, cell_maps, temporal_weight)
    queries, key_rows, value_rows = project_rows(
        residual_cols, query_weight, key_weight, value_weight
    )
    attended_cols = attend_whole(queries, key_rows, value_rows, length)
    valid_all = (jnp.arange(frames_all, dtype=jnp.int32) < length).astype(jnp.float32)
    encoded_cols = finish_rows(residual_cols, attended_cols, out_weight, valid_all)
    encoded = lax.all_to_all(encoded_cols, "frame", split_axis=0, concat_axis=2, tiled=True)
    squares = jnp.sum(jnp.square(encoded.astype(jnp.float32)))
    grand_total = lax.psum(squares, ("scene", "frame"))
    slot_count = float(lax.axis_size("scene") * lax.axis_size("frame") * f_dev * CELLS * C2)
    kl_loss = 0.5 * grand_total / slot_count
    return (encoded[None], kl_loss)


def solution(mesh):
    placed = (P("scene", "frame", None, None), P("scene"), P(), P(), P(), P(), P(), P(), P())
    return jax.shard_map(
        shards,
        mesh=mesh,
        in_specs=placed,
        out_specs=(P("scene", "frame", None, None), P()),
        check_vma=False,
    )
```

profile of v0, /device:TPU:0, one launch (start us, length us, event | category | flops | bytes accessed | tf_op | source)
XLA Modules:
  0.0 175.9 jit_solution(6949162272916972994)
XLA Ops:
  0.6 0.0 copy-start
  1.3 2.6 %copy.50 = bf16[256,3456]{0,1:T(8,128)(2,1)S(1)} copy(bf16[256,3456]{1,0:T(8,128)(2,1)} %param.12) | data formatting | bytes 3538944 | tf_op args[3]
  4.0 0.0 copy-start.2
  4.0 2.9 %reshape.52 = bf16[256,128,3,3,3]{0,4,3,2,1:T(4,128)(2,1)} reshape(bf16[256,3456]{0,1:T(8,128)(2,1)S(1)} %copy.50) | data formatting | bytes 3538944 | tf_op jit(solution)/shard_map/reshape | solution.py:19
  6.9 0.0 copy-done.2
  6.9 1.1 copy.47
  7.9 1.5 reshape.51
  9.4 0.0 copy-start.1
  9.4 5.0 %fusion.32 = bf16[4,128,8,8,8]{1,0,4,3,2:T(4,128)(2,1)S(1)} fusion(bf16[4,64,16,16,8]{1,4,3,2,0:T(8,128)(2,1)S(1)} %bitcast.108, bf16[128,64,3,3,3]{0,4,3,2,1:T(4,128)(2,1)S(1)} %reshape.51), kind=kOutput, calls=%fused_computation.44 | convolution fusion | flops 764018688 | bytes 2015232 | tf_op jit(solution)/shard_map/conv_general_dilated | solution.py:20
  14.4 0.0 copy-done.1
  14.4 6.6 %divide_multiply_fusion = f32[4,256,8,8,8]{1,0,4,3,2:T(4,128)S(1)} fusion(bf16[4,128,8,8,8]{1,0,4,3,2:T(4,128)(2,1)S(1)} %fusion.32, bf16[256,128,3,3,3]{0,4,3,2,1:T(4,128)(2,1)S(1)} %copy-done.1), kind=kOutput, calls=%fused_computation.6 | convolution fusion | flops 2793406464 | bytes 4390912 | tf_op jit(solution)/shard_map/conv_general_dilated | solution.py:20
  21.1 1.5 fusion.13
  22.6 0.0 copy-start.3
  22.6 7.4 %all-to-all-start = ((bf16[4,256,512]{1,0,2:T(4,128)(2,1)}), bf16[4,256,512]{1,0,2:T(4,128)(2,1)S(1)}, u32[]{:S(2)}, u32[]{:S(2)}) async-start(bf16[4,256,512]{1,0,2:T(4,128)(2,1)} %fusion.13), calls=%async_computation | async-start | bytes 2097152 | tf_op jit(solution)/shard_map/all_to_all | solution.py:120
  30.0 25.8 %all-to-all-done = bf16[4,256,512]{1,0,2:T(4,128)(2,1)S(1)} async-done(((bf16[4,256,512]{1,0,2:T(4,128)(2,1)}), bf16[4,256,512]{1,0,2:T(4,128)(2,1)S(1)}, u32[]{:S(2)}, u32[]{:S(2)}) %all-to-all-start) | async-done | bytes 1048608 | tf_op jit(solution)/shard_map/all_to_all | solution.py:120
  55.8 0.2 copy.52
  56.0 0.0 copy-done.3
  56.0 0.5 fusion.45
  56.4 0.5 fusion.47
  56.9 1.2 fusion.2
  58.1 0.0 copy-done
  58.1 1.5 fusion.26
  59.6 0.0 copy-start.4
  59.6 3.4 %reshape.55 = bf16[32,4,64,64]{2,1,3,0:T(4,128)(2,1)S(1)} reshape(bf16[32,256,64]{1,2,0:T(8,128)(2,1)} %fusion.26) | data formatting | bytes 2097152 | tf_op jit(solution)/shard_map/reshape | solution.py:61
  62.9 0.0 copy-done.4
  62.9 1.5 fusion.27
  64.4 4.4 %reshape.56 = bf16[32,4,64,64]{2,1,3,0:T(4,128)(2,1)} reshape(bf16[32,256,64]{1,2,0:T(8,128)(2,1)} %fusion.27) | data formatting | bytes 2097152 | tf_op jit(solution)/shard_map/reshape | solution.py:56
  68.8 8.1 %fusion.15 = f32[4,64,32,32]{3,2,1,0:T(8,128)} fusion(bf16[32,4,64,64]{2,1,3,0:T(4,128)(2,1)} %reshape.56, bf16[32,4,64,64]{2,1,3,0:T(4,128)(2,1)S(1)} %reshape.55), kind=kOutput, calls=%fused_computation.25 | convolution fusion | flops 33554432 | bytes 3145728 | tf_op jit(solution)/shard_map/qhdc,khdc->qkhc/dot_general | solution.py:81
  77.0 4.6 %copy.55 = f32[4,64,32,32]{1,2,0,3:T(8,128)S(1)} copy(f32[4,64,32,32]{3,2,1,0:T(8,128)} %fusion.15) | data formatting | bytes 2097152 | tf_op jit(solution)/shard_map/qhdc,khdc->qkhc/dot_general | solution.py:81
  81.6 1.9 %fusion.55 = (f32[32,4,64]{2,1,0:T(4,128)S(1)}, bf16[32,32,4,64]{3,1,2,0:T(8,128)(2,1)}) fusion(f32[4,64,32,32]{1,2,0,3:T(8,128)S(1)} %copy.55, pred[32]{0:T(512)(128)(4,1)S(1)} %get-tuple-element.13), kind=kOutput, calls=%fused_computation.65 | output fusion | flops 2097183 | bytes 1605664 | tf_op jit(solution)/shard_map/sub | solution.py:87
  83.5 0.0 copy-start.5
  83.5 4.8 %copy.57 = bf16[32,32,4,64]{1,0,3,2:T(8,128)(2,1)} copy(bf16[32,32,4,64]{3,1,2,0:T(8,128)(2,1)} %get-tuple-element.9) | data formatting | bytes 1048576 | tf_op jit(solution)/shard_map/convert_element_type | solution.py:91
  88.3 0.1 copy.58
  88.4 0.0 copy-done.5
  88.4 0.5 fusion.25
  88.9 1.8 %reshape.54 = bf16[32,4,64,64]{2,1,3,0:T(4,128)(2,1)} reshape(bf16[32,256,64]{1,2,0:T(8,128)(2,1)S(1)} %fusion.25) | data formatting | bytes 2097152 | tf_op jit(solution)/shard_map/reshape | solution.py:66
  90.7 7.1 %fusion.1 = bf16[32,4,64,64]{2,0,3,1:T(8,128)(2,1)S(1)} fusion(bf16[32,32,4,64]{1,0,3,2:T(8,128)(2,1)} %copy.57, bf16[32,4,64,64]{2,1,3,0:T(4,128)(2,1)} %reshape.54, f32[32,4,64]{0,2,1:T(8,128)S(1)} %copy.58), kind=kOutput, calls=%fused_computation.2 | convolution fusion | flops 34603008 | bytes 2654208 | tf_op jit(solution)/shard_map/qkhc,khdc->qhdc/dot_general | solution.py:89
  97.8 1.6 copy.59
  99.4 0.0 copy-start.6
  99.4 2.2 %reshape.57 = bf16[32,256,64]{1,2,0:T(8,128)(2,1)} reshape(bf16[32,4,64,64]{2,1,3,0:T(4,128)(2,1)S(1)} %copy.59) | data formatting | bytes 2097152 | tf_op jit(solution)/shard_map/reshape | solution.py:75
  101.6 0.0 copy-done.6
  101.6 1.7 fusion.5
  103.3 29.3 %all_to_all.33 = bf16[32,256,64]{1,2,0:T(8,128)(2,1)S(1)} all-to-all(bf16[32,256,64]{1,2,0:T(8,128)(2,1)S(1)} %fusion.5), channel_id=1, replica_groups=mesh['scene'=4,'frame'=8] {'frame'}, dimensions={0} | all-to-all | bytes 2097152 | tf_op jit(solution)/shard_map/all_to_all | solution.py:130
  132.6 0.1 copy.60
  132.7 1.1 multiply_reduce_fusion
  133.8 1.3 copy.61
  135.1 39.0 %psum.7 = f32[]{:T(128)} all-reduce(f32[]{:T(128)} %multiply_reduce_fusion), channel_id=1, replica_groups=mesh['scene'=4,'frame'=8] {'scene','frame'}, use_global_device_ids=true, to_apply=%region_4.5 | all-reduce | flops 1 | bytes 8 | tf_op jit(solution)/shard_map/psum | solution.py:132
  (3 shorter events, 0.0 us)
Async XLA Ops:
  0.6 57.5 %copy-start = (bf16[256,256]{1,0:T(8,128)(2,1)S(1)}, bf16[256,256]{1,0:T(8,128)(2,1)}, u32[]{:S(2)}) copy-start(bf16[256,256]{1,0:T(8,128)(2,1)} %param.15) | copy-start | bytes 393220
  4.0 2.9 %copy-start.2 = (bf16[1,4,64,2048]{3,2,1,0:T(8,128)(2,1)S(1)}, bf16[1,4,64,2048]{3,2,1,0:T(8,128)(2,1)}, u32[]{:S(2)}) copy-start(bf16[1,4,64,2048]{3,2,1,0:T(8,128)(2,1)} %param.9) | copy-start | bytes 3145732
  9.4 5.0 %copy-start.1 = (bf16[256,128,3,3,3]{0,4,3,2,1:T(4,128)(2,1)S(1)}, bf16[256,128,3,3,3]{0,4,3,2,1:T(4,128)(2,1)}, u32[]{:S(2)}) copy-start(bf16[256,128,3,3,3]{0,4,3,2,1:T(4,128)(2,1)} %reshape.52) | copy-start | bytes 5308420
  22.6 33.4 %copy-start.3 = (bf16[3,256,256]{2,1,0:T(8,128)(2,1)S(1)}, bf16[3,256,256]{2,1,0:T(8,128)(2,1)}, u32[]{:S(2)}) copy-start(bf16[3,256,256]{2,1,0:T(8,128)(2,1)} %param.13) | copy-start | bytes 1179652
  22.6 33.2 %all-to-all-start = ((bf16[4,256,512]{1,0,2:T(4,128)(2,1)}), bf16[4,256,512]{1,0,2:T(4,128)(2,1)S(1)}, u32[]{:S(2)}, u32[]{:S(2)}) async-start(bf16[4,256,512]{1,0,2:T(4,128)(2,1)} %fusion.13), calls=%async_computation | async-start | bytes 2097152 | tf_op jit(solution)/shard_map/all_to_all | solution.py:120
  59.6 3.4 %copy-start.4 = (bf16[256,256]{1,0:T(8,128)(2,1)S(1)}, bf16[256,256]{1,0:T(8,128)(2,1)}, u32[]{:S(2)}) copy-start(bf16[256,256]{1,0:T(8,128)(2,1)} %param.14) | copy-start | bytes 393220
  83.5 4.9 %copy-start.5 = (bf16[256,256]{1,0:T(8,128)(2,1)S(1)}, bf16[256,256]{1,0:T(8,128)(2,1)}, u32[]{:S(2)}) copy-start(bf16[256,256]{1,0:T(8,128)(2,1)} %param.16) | copy-start | bytes 393220
  99.4 2.2 %copy-start.6 = (bf16[256,256]{1,0:T(8,128)(2,1)S(1)}, bf16[256,256]{1,0:T(8,128)(2,1)}, u32[]{:S(2)}) copy-start(bf16[256,256]{1,0:T(8,128)(2,1)} %param.17) | copy-start | bytes 393220
where the time goes:
time: 176 us
  blocking collectives  68.2 us (39%)
  matrix products  34 us (19%)
  local copies, waits for them, and re-layouts  32.5 us (18%)
  waiting for transfers between devices  25.8 us (15%)
  starting transfers between devices  7.41 us (4%)
  other arithmetic  4.62 us (3%)
  between operations  3.32 us (2%)
    psum x1, blocking collectives, shards(): grand_total = lax.psum(squares, ('scene', 'frame'))  39 us
    all_to_all x1, blocking collectives, shards(): lax.all_to_all(encoded_cols, 'frame', split_axis=0, concat_axis=2, tiled=...  29.3 us
    all_to_all x1, waiting for transfers between devices, shards(): lax.all_to_all(second_maps, 'frame', split_axis=2, concat_axis=0, tiled=T...  25.8 us
    conv_general_dilated x2, matrix products, spatial_conv(): lax.conv_general_dilated(voxels, kernel, (stride, stride, 1), ((1, 1), (1...  11.6 us
    dot_general x1, matrix products, attend_whole(): jnp.einsum('qhdc,khdc->qkhc', queries, key_rows, preferred_element_type=j...  8.13 us
    all_to_all x1, starting transfers between devices, shards(): lax.all_to_all(second_maps, 'frame', split_axis=2, concat_axis=0, tiled=T...  7.41 us
    dot_general x7, matrix products, mix_channels(): jnp.einsum('oc,fcn->fon', weight, maps, preferred_element_type=jnp.float32)  7.2 us
    dot_general x1, matrix products, attend_whole(): jnp.einsum('qkhc,khdc->qhdc', raw_weights.astype(jnp.bfloat16), value_row...  7.06 us
  transfers between devices with their start and end apart: 1, of which 1 were waited for; matrix products, arithmetic and copies ran while one was open for 0% of the time, Pallas kernels for 0%

commit v1 on v0

--- a/solution.py
+++ b/solution.py
@@ -12,6 +12,18 @@
 ZD = 8
 CELLS = 512
 NORM_EPS = 1e-06
+
+
+def exchange_directly(value, axis, split, join):
+    ways, here = (lax.axis_size(axis), lax.axis_index(axis))
+    width = value.shape[split] // ways
+    turned = jnp.roll(value, -here * width, axis=split)
+    got = [lax.slice_in_dim(turned, 0, width, axis=split)]
+    for far in range(1, ways):
+        sent = lax.slice_in_dim(turned, far * width, (far + 1) * width, axis=split)
+        got.append(lax.ppermute(sent, axis, [(d, (d + far) % ways) for d in range(ways)]))
+    line = jnp.concatenate(got[::-1], axis=join)
+    return jnp.roll(line, (here + 1) * got[0].shape[join], axis=join)
 
 
 def spatial_conv(voxels, weight, channels_in, stride):
@@ -117,7 +129,7 @@
     second_maps = (second_full.reshape(f_dev, C2, CELLS) * valid_rows[:, None, None]).astype(
         jnp.bfloat16
     )
-    cell_maps = lax.all_to_all(second_maps, "frame", split_axis=2, concat_axis=0, tiled=True)
+    cell_maps = exchange_directly(second_maps, "frame", 2, 0)
     frames_all = cell_maps.shape[0]
     padded_all = jnp.pad(cell_maps, ((1, 1), (0, 0), (0, 0)))
     residual_cols = temporal_block(padded_all, cell_maps, temporal_weight)

time: 176 us -> 174 us (0.989)
  waiting for transfers between devices: 25.8 us -> 18.9 us
  starting transfers between devices: 7.41 us -> 11 us
    all_to_all x1 -> x0, waiting for transfers between devices: 25.8 us -> none  [shards(): lax.all_to_all(second_maps, 'frame', split_axis=2, concat_axis=0, tiled=T...]
    ppermute x0 -> x7, waiting for transfers between devices: none -> 18.9 us  [exchange_directly(): lax.ppermute(sent, axis, [(d, (d + far) % ways) for d in range(ways)])]
    ppermute x0 -> x7, starting transfers between devices: none -> 11 us  [exchange_directly(): lax.ppermute(sent, axis, [(d, (d + far) % ways) for d in range(ways)])]
    all_to_all x1 -> x0, starting transfers between devices: 7.41 us -> none  [shards(): lax.all_to_all(second_maps, 'frame', split_axis=2, concat_axis=0, tiled=T...]
    unnamed x17 -> x32, local copies, waits for them, and re-layouts: 5.04 us -> 6.93 us
  transfers between devices with their start and end apart: 1 -> 7, of which waited for: 1 -> 5; matrix products, arithmetic and copies ran while one was open for 0% -> 0% of each run, Pallas kernels for 0% -> 0%
where the time goes in v1:
time: 174 us
  blocking collectives  68.1 us (39%)
  matrix products  34.9 us (20%)
  local copies, waits for them, and re-layouts  32.8 us (19%)
  waiting for transfers between devices  18.9 us (11%)
  starting transfers between devices  11 us (6%)
  other arithmetic  4.69 us (3%)
  between operations  3.43 us (2%)
    psum x1, blocking collectives, shards(): grand_total = lax.psum(squares, ('scene', 'frame'))  39 us
    all_to_all x1, blocking collectives, shards(): lax.all_to_all(encoded_cols, 'frame', split_axis=0, concat_axis=2, tiled=...  29.1 us
    ppermute x7, waiting for transfers between devices, exchange_directly(): lax.ppermute(sent, axis, [(d, (d + far) % ways) for d in range(ways)])  18.9 us
    conv_general_dilated x2, matrix products, spatial_conv(): lax.conv_general_dilated(voxels, kernel, (stride, stride, 1), ((1, 1), (1...  12.5 us
    ppermute x7, starting transfers between devices, exchange_directly(): lax.ppermute(sent, axis, [(d, (d + far) % ways) for d in range(ways)])  11 us
    dot_general x1, matrix products, attend_whole(): jnp.einsum('qhdc,khdc->qkhc', queries, key_rows, preferred_element_type=j...  8.14 us
    dot_general x7, matrix products, mix_channels(): jnp.einsum('oc,fcn->fon', weight, maps, preferred_element_type=jnp.float32)  7.21 us
    dot_general x1, matrix products, attend_whole(): jnp.einsum('qkhc,khdc->qhdc', raw_weights.astype(jnp.bfloat16), value_row...  7.07 us
  transfers between devices with their start and end apart: 7, of which 5 were waited for; matrix products, arithmetic and copies ran while one was open for 0% of the time, Pallas kernels for 0%

profile of v1, /device:TPU:0, one launch (start us, length us, event | category | flops | bytes accessed | tf_op | source)
XLA Modules:
  0.0 173.8 jit_solution(8046543520992738304)
XLA Ops:
  0.6 0.0 copy-start
  0.6 0.0 copy-start.2
  0.7 2.8 %copy.47 = bf16[1,4,64,2048]{2,3,1,0:T(8,128)(2,1)} copy(bf16[1,4,64,2048]{3,2,1,0:T(8,128)(2,1)} %param.9) | data formatting | bytes 2097152 | tf_op args[0]
  3.5 0.0 copy-done.2
  3.5 0.2 reshape.51
  3.7 2.6 %copy.50 = bf16[256,3456]{0,1:T(8,128)(2,1)S(1)} copy(bf16[256,3456]{1,0:T(8,128)(2,1)} %param.12) | data formatting | bytes 3538944 | tf_op args[3]
  6.3 2.9 %reshape.52 = bf16[256,128,3,3,3]{0,4,3,2,1:T(4,128)(2,1)} reshape(bf16[256,3456]{0,1:T(8,128)(2,1)S(1)} %copy.50) | data formatting | bytes 3538944 | tf_op jit(solution)/shard_map/reshape | solution.py:31
  9.9 0.0 copy-start.1
  9.9 5.9 %fusion.33 = bf16[4,128,8,8,8]{1,0,4,3,2:T(4,128)(2,1)S(1)} fusion(bf16[4,64,16,16,8]{1,4,3,2,0:T(8,128)(2,1)} %bitcast.94, bf16[128,64,3,3,3]{0,4,3,2,1:T(4,128)(2,1)S(1)} %reshape.51), kind=kOutput, calls=%fused_computation.47 | convolution fusion | flops 764018688 | bytes 2015232 | tf_op jit(solution)/shard_map/conv_general_dilated | solution.py:32
  15.8 0.0 copy-done.1
  15.8 6.6 %divide_multiply_fusion = f32[4,256,8,8,8]{1,0,4,3,2:T(4,128)S(1)} fusion(bf16[4,128,8,8,8]{1,0,4,3,2:T(4,128)(2,1)S(1)} %fusion.33, bf16[256,128,3,3,3]{0,4,3,2,1:T(4,128)(2,1)S(1)} %copy-done.1), kind=kOutput, calls=%fused_computation.6 | convolution fusion | flops 2793406464 | bytes 4390912 | tf_op jit(solution)/shard_map/conv_general_dilated | solution.py:32
  22.4 0.6 fusion.17
  23.0 1.0 fusion.30
  24.0 0.1 fusion.66
  24.1 6.1 %collective-permute-start = (bf16[4,256,64]{1,2,0:T(8,128)(2,1)S(1)}, bf16[4,256,64]{1,2,0:T(8,128)(2,1)S(1)}, u32[]{:S(2)}, u32[]{:S(2)}) collective-permute-start(bf16[4,256,64]{1,2,0:T(8,128)(2,1)S(1)} %get-tuple-element.16), channel_id=1, source_target_pairs={{0,7},{1,0},{2,1},{3,2},{4,3},{5,4},{6,5},{7,6},{8,15},{9,8},{10,9... | collective-permute-start | bytes 393224 | tf_op jit(solution)/shard_map/ppermute | solution.py:24
  30.2 0.4 collective-permute-start.1
  30.6 0.0 collective-permute-start.2
  30.6 3.0 %collective-permute-start.3 = (bf16[4,256,64]{1,2,0:T(8,128)(2,1)S(1)}, bf16[4,256,64]{1,2,0:T(8,128)(2,1)S(1)}, u32[]{:S(2)}, u32[]{:S(2)}) collective-permute-start(bf16[4,256,64]{1,2,0:T(8,128)(2,1)S(1)} %get-tuple-element.13), channel_id=1, source_target_pairs={{0,4},{1,5},{2,6},{3,7},{4,0},{5,1},{6,2},{7,3},{8,12},{9,13},{10,... | collective-permute-start | bytes 393224 | tf_op jit(solution)/shard_map/ppermute | solution.py:24
  33.6 0.0 collective-permute-start.4
  33.6 0.5 collective-permute-done
  34.1 0.0 copy-start.3
  34.1 1.4 collective-permute-start.5
  35.5 1.4 collective-permute-done.1
  36.9 0.0 collective-permute-start.6
  37.0 2.8 %collective-permute-done.2 = bf16[4,256,64]{1,2,0:T(8,128)(2,1)S(1)} collective-permute-done((bf16[4,256,64]{1,2,0:T(8,128)(2,1)S(1)}, bf16[4,256,64]{1,2,0:T(8,128)(2,1)S(1)}, u32[]{:S(2)}, u32[]{:S(2)}) %collective-permute-start.2) | collective-permute-done | bytes 131104 | tf_op jit(solution)/shard_map/ppermute | solution.py:24
  39.8 12.7 %collective-permute-done.3 = bf16[4,256,64]{1,2,0:T(8,128)(2,1)S(1)} collective-permute-done((bf16[4,256,64]{1,2,0:T(8,128)(2,1)S(1)}, bf16[4,256,64]{1,2,0:T(8,128)(2,1)S(1)}, u32[]{:S(2)}, u32[]{:S(2)}) %collective-permute-start.3) | collective-permute-done | bytes 131104 | tf_op jit(solution)/shard_map/ppermute | solution.py:24
  52.5 1.6 collective-permute-done.4
  54.1 0.0 collective-permute-done.5
  54.1 0.0 collective-permute-done.6
  54.3 0.0 copy-done.3
  54.3 0.5 fusion.40
  54.8 0.5 fusion.42
  55.3 1.1 fusion.2
  56.5 0.0 copy-done
  56.5 1.5 fusion.27
  57.9 0.0 copy-start.4
  57.9 3.4 %reshape.56 = bf16[32,4,64,64]{2,1,3,0:T(4,128)(2,1)S(1)} reshape(bf16[32,256,64]{1,2,0:T(8,128)(2,1)} %fusion.27) | data formatting | bytes 2097152 | tf_op jit(solution)/shard_map/reshape | solution.py:68
  61.3 0.0 copy-done.4
  61.3 1.5 fusion.26
  62.8 4.4 %reshape.55 = bf16[32,4,64,64]{2,1,3,0:T(4,128)(2,1)} reshape(bf16[32,256,64]{1,2,0:T(8,128)(2,1)} %fusion.26) | data formatting | bytes 2097152 | tf_op jit(solution)/shard_map/reshape | solution.py:73
  67.2 8.1 %fusion.14 = f32[4,64,32,32]{3,2,1,0:T(8,128)} fusion(bf16[32,4,64,64]{2,1,3,0:T(4,128)(2,1)S(1)} %reshape.56, bf16[32,4,64,64]{2,1,3,0:T(4,128)(2,1)} %reshape.55), kind=kOutput, calls=%fused_computation.25 | convolution fusion | flops 33554432 | bytes 3145728 | tf_op jit(solution)/shard_map/qhdc,khdc->qkhc/dot_general | solution.py:93
  75.3 4.4 %copy.55 = f32[4,64,32,32]{1,2,0,3:T(8,128)S(1)} copy(f32[4,64,32,32]{3,2,1,0:T(8,128)} %fusion.14) | data formatting | bytes 2097152 | tf_op jit(solution)/shard_map/qhdc,khdc->qkhc/dot_general | solution.py:93
  79.7 1.9 %fusion.65 = (f32[32,4,64]{2,1,0:T(4,128)S(1)}, bf16[32,32,4,64]{3,1,2,0:T(8,128)(2,1)}) fusion(f32[4,64,32,32]{1,2,0,3:T(8,128)S(1)} %copy.55, pred[32]{0:T(512)(128)(4,1)S(1)} %get-tuple-element.20), kind=kOutput, calls=%fused_computation.91 | output fusion | flops 2097183 | bytes 1605664 | tf_op jit(solution)/shard_map/sub | solution.py:99
  81.6 0.0 copy-start.5
  81.6 4.8 %copy.57 = bf16[32,32,4,64]{1,0,3,2:T(8,128)(2,1)} copy(bf16[32,32,4,64]{3,1,2,0:T(8,128)(2,1)} %get-tuple-element.9) | data formatting | bytes 1048576 | tf_op jit(solution)/shard_map/convert_element_type | solution.py:103
  86.4 0.0 copy-done.5
  86.4 0.5 fusion.25
  86.9 1.8 %reshape.54 = bf16[32,4,64,64]{2,1,3,0:T(4,128)(2,1)} reshape(bf16[32,256,64]{1,2,0:T(8,128)(2,1)S(1)} %fusion.25) | data formatting | bytes 2097152 | tf_op jit(solution)/shard_map/reshape | solution.py:78
  88.7 0.1 copy.58
  88.8 7.1 %fusion.1 = bf16[32,4,64,64]{2,0,3,1:T(8,128)(2,1)S(1)} fusion(bf16[32,32,4,64]{1,0,3,2:T(8,128)(2,1)} %copy.57, bf16[32,4,64,64]{2,1,3,0:T(4,128)(2,1)} %reshape.54, f32[32,4,64]{0,2,1:T(8,128)S(1)} %copy.58), kind=kOutput, calls=%fused_computation.2 | convolution fusion | flops 34603008 | bytes 2654208 | tf_op jit(solution)/shard_map/qkhc,khdc->qhdc/dot_general | solution.py:101
  95.9 1.6 copy.59
  97.5 0.0 copy-start.6
  97.6 2.2 %reshape.57 = bf16[32,256,64]{1,2,0:T(8,128)(2,1)} reshape(bf16[32,4,64,64]{2,1,3,0:T(4,128)(2,1)S(1)} %copy.59) | data formatting | bytes 2097152 | tf_op jit(solution)/shard_map/reshape | solution.py:87
  99.7 0.0 copy-done.6
  99.7 1.7 fusion.5
  101.4 29.1 %all_to_all.15 = bf16[32,256,64]{1,2,0:T(8,128)(2,1)S(1)} all-to-all(bf16[32,256,64]{1,2,0:T(8,128)(2,1)S(1)} %fusion.5), channel_id=1, replica_groups=mesh['scene'=4,'frame'=8] {'frame'}, dimensions={0} | all-to-all | bytes 2097152 | tf_op jit(solution)/shard_map/all_to_all | solution.py:142
  130.5 0.1 copy.60
  130.7 1.1 multiply_reduce_fusion
  131.8 1.3 copy.61
  133.1 39.0 %psum.7 = f32[]{:T(128)} all-reduce(f32[]{:T(128)} %multiply_reduce_fusion), channel_id=1, replica_groups=mesh['scene'=4,'frame'=8] {'scene','frame'}, use_global_device_ids=true, to_apply=%region_4.5 | all-reduce | flops 1 | bytes 8 | tf_op jit(solution)/shard_map/psum | solution.py:144
  (19 shorter events, 0.2 us)
Async XLA Ops:
  0.6 55.8 %copy-start = (bf16[256,256]{1,0:T(8,128)(2,1)S(1)}, bf16[256,256]{1,0:T(8,128)(2,1)}, u32[]{:S(2)}) copy-start(bf16[256,256]{1,0:T(8,128)(2,1)} %param.14) | copy-start | bytes 393220
  0.6 2.8 %copy-start.2 = (bf16[128,1728]{0,1:T(8,128)(2,1)S(1)}, bf16[128,1728]{0,1:T(8,128)(2,1)}, u32[]{:S(2)}) copy-start(bf16[128,1728]{0,1:T(8,128)(2,1)} %param.11) | copy-start | bytes 1327108
  9.9 5.9 %copy-start.1 = (bf16[256,128,3,3,3]{0,4,3,2,1:T(4,128)(2,1)S(1)}, bf16[256,128,3,3,3]{0,4,3,2,1:T(4,128)(2,1)}, u32[]{:S(2)}) copy-start(bf16[256,128,3,3,3]{0,4,3,2,1:T(4,128)(2,1)} %reshape.52) | copy-start | bytes 5308420
  24.1 10.0 %collective-permute-start = (bf16[4,256,64]{1,2,0:T(8,128)(2,1)S(1)}, bf16[4,256,64]{1,2,0:T(8,128)(2,1)S(1)}, u32[]{:S(2)}, u32[]{:S(2)}) collective-permute-start(bf16[4,256,64]{1,2,0:T(8,128)(2,1)S(1)} %get-tuple-element.16), channel_id=1, source_target_pairs={{0,7},{1,0},{2,1},{3,2},{4,3},{5,4},{6,5},{7,6},{8,15},{9,8},{10,9... | collective-permute-start | bytes 393224 | tf_op jit(solution)/shard_map/ppermute | solution.py:24
  30.2 6.8 %collective-permute-start.1 = (bf16[4,256,64]{1,2,0:T(8,128)(2,1)S(1)}, bf16[4,256,64]{1,2,0:T(8,128)(2,1)S(1)}, u32[]{:S(2)}, u32[]{:S(2)}) collective-permute-start(bf16[4,256,64]{1,2,0:T(8,128)(2,1)S(1)} %get-tuple-element.15), channel_id=1, source_target_pairs={{0,6},{1,7},{2,0},{3,1},{4,2},{5,3},{6,4},{7,5},{8,14},{9,15},{10,... | collective-permute-start | bytes 393224 | tf_op jit(solution)/shard_map/ppermute | solution.py:24
  30.6 9.1 %collective-permute-start.2 = (bf16[4,256,64]{1,2,0:T(8,128)(2,1)S(1)}, bf16[4,256,64]{1,2,0:T(8,128)(2,1)S(1)}, u32[]{:S(2)}, u32[]{:S(2)}) collective-permute-start(bf16[4,256,64]{1,2,0:T(8,128)(2,1)S(1)} %get-tuple-element.14), channel_id=1, source_target_pairs={{0,5},{1,6},{2,7},{3,0},{4,1},{5,2},{6,3},{7,4},{8,13},{9,14},{10,... | collective-permute-start | bytes 393224 | tf_op jit(solution)/shard_map/ppermute | solution.py:24
  30.6 21.9 %collective-permute-start.3 = (bf16[4,256,64]{1,2,0:T(8,128)(2,1)S(1)}, bf16[4,256,64]{1,2,0:T(8,128)(2,1)S(1)}, u32[]{:S(2)}, u32[]{:S(2)}) collective-permute-start(bf16[4,256,64]{1,2,0:T(8,128)(2,1)S(1)} %get-tuple-element.13), channel_id=1, source_target_pairs={{0,4},{1,5},{2,6},{3,7},{4,0},{5,1},{6,2},{7,3},{8,12},{9,13},{10,... | collective-permute-start | bytes 393224 | tf_op jit(solution)/shard_map/ppermute | solution.py:24
  33.6 20.4 %collective-permute-start.4 = (bf16[4,256,64]{1,2,0:T(8,128)(2,1)S(1)}, bf16[4,256,64]{1,2,0:T(8,128)(2,1)S(1)}, u32[]{:S(2)}, u32[]{:S(2)}) collective-permute-start(bf16[4,256,64]{1,2,0:T(8,128)(2,1)S(1)} %get-tuple-element.12), channel_id=1, source_target_pairs={{0,3},{1,4},{2,5},{3,6},{4,7},{5,0},{6,1},{7,2},{8,11},{9,12},{10,... | collective-permute-start | bytes 393224 | tf_op jit(solution)/shard_map/ppermute | solution.py:24
  34.1 20.2 %copy-start.3 = (bf16[3,256,256]{2,1,0:T(8,128)(2,1)S(1)}, bf16[3,256,256]{2,1,0:T(8,128)(2,1)}, u32[]{:S(2)}) copy-start(bf16[3,256,256]{2,1,0:T(8,128)(2,1)} %param.13) | copy-start | bytes 1179652
  34.1 20.0 %collective-permute-start.5 = (bf16[4,256,64]{1,2,0:T(8,128)(2,1)S(1)}, bf16[4,256,64]{1,2,0:T(8,128)(2,1)S(1)}, u32[]{:S(2)}, u32[]{:S(2)}) collective-permute-start(bf16[4,256,64]{1,2,0:T(8,128)(2,1)S(1)} %get-tuple-element.11), channel_id=1, source_target_pairs={{0,2},{1,3},{2,4},{3,5},{4,6},{5,7},{6,0},{7,1},{8,10},{9,11},{10,... | collective-permute-start | bytes 393224 | tf_op jit(solution)/shard_map/ppermute | solution.py:24
  36.9 17.2 %collective-permute-start.6 = (bf16[4,256,64]{1,2,0:T(8,128)(2,1)S(1)}, bf16[4,256,64]{1,2,0:T(8,128)(2,1)S(1)}, u32[]{:S(2)}, u32[]{:S(2)}) collective-permute-start(bf16[4,256,64]{1,2,0:T(8,128)(2,1)S(1)} %get-tuple-element.10), channel_id=1, source_target_pairs={{0,1},{1,2},{2,3},{3,4},{4,5},{5,6},{6,7},{7,0},{8,9},{9,10},{10,1... | collective-permute-start | bytes 393224 | tf_op jit(solution)/shard_map/ppermute | solution.py:24
  57.9 3.4 %copy-start.4 = (bf16[256,256]{1,0:T(8,128)(2,1)S(1)}, bf16[256,256]{1,0:T(8,128)(2,1)}, u32[]{:S(2)}) copy-start(bf16[256,256]{1,0:T(8,128)(2,1)} %param.15) | copy-start | bytes 393220
  81.6 4.8 %copy-start.5 = (bf16[256,256]{1,0:T(8,128)(2,1)S(1)}, bf16[256,256]{1,0:T(8,128)(2,1)}, u32[]{:S(2)}) copy-start(bf16[256,256]{1,0:T(8,128)(2,1)} %param.16) | copy-start | bytes 393220
  97.5 2.2 %copy-start.6 = (bf16[256,256]{1,0:T(8,128)(2,1)S(1)}, bf16[256,256]{1,0:T(8,128)(2,1)}, u32[]{:S(2)}) copy-start(bf16[256,256]{1,0:T(8,128)(2,1)} %param.17) | copy-start | bytes 393220
